TPU v7x, 512 devices: a whole 4x4x16 slice. The times are simulated.
512 devices in a mesh: seq: 128 (over x, z, core), head: 4 (over y).
Axes of the slice: x: 4, y: 4, z: 16, core: 2. Of those that a mesh axis runs over, the one named last changes fastest.
Arguments:
- tokens: bfloat16 [128, 128, 2048], P('seq'), may hold values from -6 to 6
- attn_gain: bfloat16 [2048], replicated, may hold values from 0.099609375 to 1.8984375
- q_gain: bfloat16 [64], replicated, may hold values from 0.099609375 to 1.8984375
- k_gain: bfloat16 [64], replicated, may hold values from 0.099609375 to 1.8984375
- ffn_gain: bfloat16 [2048], replicated, may hold values from 0.099609375 to 1.8984375
- w_query: bfloat16 [2048, 1280], P('seq', 'head'), may hold values from -0.125 to 0.125
- w_keyval: bfloat16 [2048, 640], P('seq'), may hold values from -0.125 to 0.125
- w_out: bfloat16 [1280, 2048], P('head', 'seq'), may hold values from -0.15625 to 0.15625
- prior_cache: bfloat16 [128, 512, 640], P(None, 'seq')
- prior_len: int32 [128], replicated, may hold values from 0 to 512, as said below
- stretch_len: int32 [128], replicated, may hold values from 1 to 128, as said below
Outputs:
- hidden: bfloat16 [128, 128, 2048], P('seq', 'head')
- ffn_input: bfloat16 [128, 128, 2048], P('seq', 'head')
- new_cache: bfloat16 [128, 128, 640], P('seq', 'head')
- decode_cache: bfloat16 [128, 512, 640], P('seq', 'head')
Inputs may be any that keep to these rules, and one draw needn't show every extreme that they name: `prior_len`: some request has all 512 slots in use. `stretch_len`: some request fills its stretch.
All inputs are finite; a program needn't handle non-finite values.
Results may differ from a plain program's by a relative error of at most 0.011.
The roundings to bfloat16 on the way count: a program that leaves them out, or rounds other values in their place, can miss the bound.
Values may be sent and summed in bfloat16 or wider, within the bound.
A program may use at most 64 MiB of HBM per device.

v0:
```python
import math
import jax
import jax.numpy as jnp
from jax import lax
from jax.sharding import PartitionSpec as P

HD = 64
QH = 20
KVH = 5
epsilon = 1e-06


def rms_norm(values, gain):
    return values * lax.rsqrt(jnp.mean(values * values, axis=-1, keepdims=True) + epsilon) * gain


def rotary(values, positions):
    middle = values.shape[-1] // 2
    inverse = jnp.exp(
        jnp.arange(middle, dtype=jnp.float32) * (-2.0 * math.log(10000.0) / values.shape[-1])
    )
    angles = positions.astype(jnp.float32)[:, None] * inverse[None, :]
    cosine = jnp.concatenate([jnp.cos(angles), jnp.cos(angles)], axis=-1)[:, None, :]
    sine = jnp.concatenate([jnp.sin(angles), jnp.sin(angles)], axis=-1)[:, None, :]
    turned = jnp.concatenate([-values[..., middle:], values[..., :middle]], axis=-1)
    return values * cosine + turned * sine


def attend_dense(
    query, prior_keys, prior_values, fresh_keys, fresh_values, prior_count, score_scale
):
    length = fresh_keys.shape[0]
    stored = prior_keys.shape[0]
    all_keys = jnp.concatenate([prior_keys, fresh_keys], axis=0)
    all_values = jnp.concatenate([prior_values, fresh_values], axis=0)
    scores = (
        jnp.einsum("qhd,khd->hqk", query, all_keys, preferred_element_type=jnp.float32)
        * score_scale
    )
    offsets = jnp.arange(length, dtype=jnp.int32)
    earlier = jnp.arange(stored, dtype=jnp.int32)[None, :] < prior_count
    allowed = jnp.concatenate(
        [jnp.broadcast_to(earlier, (length, stored)), offsets[None, :] <= offsets[:, None]], axis=1
    )
    scores = jnp.where(allowed[None], scores, -jnp.inf)
    top = jnp.max(scores, axis=-1, keepdims=True)
    weights = jnp.exp(scores - top)
    total = jnp.sum(weights, axis=-1)
    mixed = jnp.einsum(
        "hqk,khd->qhd", weights.astype(jnp.bfloat16), all_values, preferred_element_type=jnp.float32
    )
    return mixed / total.T[:, :, None]


def shards(
    tokens,
    attn_gain,
    q_gain,
    k_gain,
    ffn_gain,
    w_query,
    w_keyval,
    w_out,
    prior_cache,
    prior_len,
    stretch_len,
):
    seq_index = lax.axis_index("seq")
    head_index = lax.axis_index("head")
    head_count = lax.axis_size("head")
    local_requests, length, width = tokens.shape
    token_count = local_requests * length
    width_kv = KVH * HD
    local_heads = QH // head_count
    score_scale = 1.0 / math.sqrt(HD)
    flat = tokens.reshape(token_count, width)
    normed = rms_norm(flat.astype(jnp.float32), attn_gain.astype(jnp.float32)).astype(jnp.bfloat16)
    first = jnp.dot(
        normed,
        lax.all_gather(w_query, "seq", axis=0, tiled=True),
        preferred_element_type=jnp.float32,
    )
    second = jnp.dot(
        normed,
        lax.all_gather(w_keyval, "seq", axis=0, tiled=True),
        preferred_element_type=jnp.float32,
    )
    query = first
    prior_counts = lax.dynamic_slice_in_dim(prior_len, seq_index * local_requests, local_requests)
    stretch_counts = lax.dynamic_slice_in_dim(
        stretch_len, seq_index * local_requests, local_requests
    )
    offsets = jnp.arange(length, dtype=jnp.int32)
    positions = (prior_counts[:, None] + offsets[None, :]).reshape(token_count)
    query = rotary(
        rms_norm(query.reshape(token_count, local_heads, HD), q_gain.astype(jnp.float32)), positions
    ).astype(jnp.bfloat16)
    fresh_keys = rotary(
        rms_norm(second[:, :width_kv].reshape(token_count, KVH, HD), k_gain.astype(jnp.float32)),
        positions,
    ).astype(jnp.bfloat16)
    fresh_values = second[:, width_kv:].reshape(token_count, KVH, HD).astype(jnp.bfloat16)
    gathered_cache = lax.all_to_all(prior_cache, "seq", split_axis=0, concat_axis=1, tiled=True)
    stored = gathered_cache.shape[1]
    block_slots = stored // head_count
    decode_cache = lax.dynamic_slice_in_dim(
        gathered_cache, head_index * block_slots, block_slots, 1
    )
    group = (head_index * local_heads + jnp.arange(local_heads, dtype=jnp.int32)) // (QH // KVH)
    prior_keys = jnp.take(
        gathered_cache[:, :, :width_kv].reshape(local_requests, stored, KVH, HD), group, axis=2
    )
    prior_values = jnp.take(
        gathered_cache[:, :, width_kv:].reshape(local_requests, stored, KVH, HD), group, axis=2
    )
    stretch_keys = jnp.take(fresh_keys.reshape(local_requests, length, KVH, HD), group, axis=2)
    stretch_values = jnp.take(fresh_values.reshape(local_requests, length, KVH, HD), group, axis=2)
    query_blocks = query.reshape(local_requests, length, local_heads, HD)
    mixed = attend_dense(
        query_blocks[0],
        prior_keys[0],
        prior_values[0],
        stretch_keys[0],
        stretch_values[0],
        prior_counts[0],
        score_scale,
    )
    results = mixed.astype(jnp.bfloat16).reshape(length, local_heads * HD)
    terms = jnp.dot(
        results,
        lax.all_gather(w_out, "seq", axis=1, tiled=True),
        preferred_element_type=jnp.float32,
    )
    share_rows = length // head_count
    summed = lax.psum_scatter(
        terms.reshape(local_requests, length, width).astype(jnp.bfloat16),
        "head",
        scatter_dimension=1,
        tiled=True,
    ).astype(jnp.float32)
    own_tokens = lax.dynamic_slice_in_dim(tokens, head_index * share_rows, share_rows, 1).astype(
        jnp.float32
    )
    residual = own_tokens + summed
    row_offsets = head_index * share_rows + jnp.arange(share_rows, dtype=jnp.int32)
    valid = row_offsets[None, :] < stretch_counts[:, None]
    hidden = jnp.where(valid[:, :, None], residual, 0.0).astype(jnp.bfloat16)
    ffn_input = jnp.where(
        valid[:, :, None], rms_norm(residual, ffn_gain.astype(jnp.float32)), 0.0
    ).astype(jnp.bfloat16)
    fresh = jnp.concatenate(
        [
            fresh_keys.reshape(local_requests, length, width_kv),
            fresh_values.reshape(local_requests, length, width_kv),
        ],
        axis=2,
    )
    fresh = lax.dynamic_slice_in_dim(fresh, head_index * share_rows, share_rows, 1)
    fresh = jnp.where(valid[:, :, None], fresh, jnp.zeros_like(fresh))
    return (hidden, ffn_input, fresh, decode_cache)


def solution(mesh):
    placed = (
        P("seq", None, None),
        P(),
        P(),
        P(),
        P(),
        P("seq", "head"),
        P("seq", None),
        P("head", "seq"),
        P(None, "seq", None),
        P(),
        P(),
    )
    return jax.shard_map(
        shards,
        mesh=mesh,
        in_specs=placed,
        out_specs=(
            P("seq", "head", None),
            P("seq", "head", None),
            P("seq", "head", None),
            P("seq", "head", None),
        ),
        check_vma=False,
    )
```

profile of v0, /device:TPU:2, one launch (start us, length us, event | category | flops | bytes accessed | tf_op | source)
XLA Modules:
  0.0 474.5 jit_solution(8410260316562523940)
XLA Ops:
  7.2 0.7 all-gather.6.cloned.1.call-update
  8.0 0.7 all-gather.4.cloned.1.call-update
  8.7 19.5 %all-to-all-start = ((bf16[128,4,640]{2,1,0:T(4,128)(2,1)}), bf16[128,4,640]{2,1,0:T(4,128)(2,1)S(1)}, u32[]{:S(2)}, u32[]{:S(2)}) async-start(bf16[128,4,640]{2,1,0:T(4,128)(2,1)} %param.23), calls=%async_computation | async-start | bytes 1310720 | tf_op jit(solution)/shard_map/all_to_all | solution.py:103
  28.2 0.7 all-gather.8.cloned.1.call-update
  29.0 0.7 convert_element_type.100
  29.7 0.7 convert_element_type.110
  30.3 0.7 convert_element_type.107
  31.0 1.2 dynamic_slice.17
  32.2 0.6 iota_compare_fusion.1
  33.0 0.7 add_convert_fusion
  34.1 33.9 %all-to-all-done = bf16[128,4,640]{2,1,0:T(4,128)(2,1)S(1)} async-done(((bf16[128,4,640]{2,1,0:T(4,128)(2,1)}), bf16[128,4,640]{2,1,0:T(4,128)(2,1)S(1)}, u32[]{:S(2)}, u32[]{:S(2)}) %all-to-all-start) | async-done | bytes 655392 | tf_op jit(solution)/shard_map/all_to_all | solution.py:103
  68.3 87.2 %all-gather.6.cloned.1.call-done = bf16[2048,320]{1,0:T(8,128)(2,1)} async-done(((bf16[16,320]{1,0:T(8,128)(2,1)}), bf16[2048,320]{1,0:T(8,128)(2,1)}) %all-gather.6.cloned.1.call-update) | async-done | bytes 1310736 | tf_op jit(solution)/shard_map/all_gather | solution.py:80
  155.5 1.7 copy.41
  159.5 136.3 %all-gather.4.cloned.1.call-done = bf16[2048,640]{1,0:T(8,128)(2,1)} async-done(((bf16[16,640]{1,0:T(8,128)(2,1)}), bf16[2048,640]{1,0:T(8,128)(2,1)}) %all-gather.4.cloned.1.call-update) | async-done | bytes 2621456 | tf_op jit(solution)/shard_map/all_gather | solution.py:85
  295.8 2.9 fusion.17
  301.8 133.8 %all-gather.8.cloned.1.call-done = bf16[320,2048]{0,1:T(8,128)(2,1)} async-done(((bf16[320,16]{0,1:T(8,128)(2,1)}), bf16[320,2048]{0,1:T(8,128)(2,1)}) %all-gather.8.cloned.1.call-update) | async-done | bytes 1310736 | tf_op jit(solution)/shard_map/all_gather | solution.py:131
  435.6 2.8 fusion
  438.5 0.6 dynamic_slice.15
  439.2 0.7 add_compare_fusion
  439.8 0.7 constant_dynamic-slice_fusion
  440.8 0.7 copy.44
  441.5 23.6 %reduce-scatter.2.cloned.1.call-done = bf16[1,32,2048]{2,1,0:T(8,128)(2,1)} async-done(((bf16[1,128,2048]{2,1,0:T(8,128)(2,1)}), bf16[1,32,2048]{2,1,0:T(8,128)(2,1)}) %reduce-scatter.2.cloned.1.call-update) | async-done | bytes 131088 | tf_op jit(solution)/shard_map/reduce_scatter | solution.py:135
  465.2 1.1 multiply_reduce_fusion
  466.2 1.7 select_convert_fusion
  (56 shorter events, 6.6 us)
Async XLA Ops:
  7.2 26.7 %copy-start = (bf16[1,128,2048]{2,1,0:T(8,128)(2,1)S(1)}, bf16[1,128,2048]{2,1,0:T(8,128)(2,1)}, u32[]{:S(2)}) copy-start(bf16[1,128,2048]{2,1,0:T(8,128)(2,1)} %param.15) | copy-start | bytes 1572868
  7.2 148.3 %all-gather.6.cloned.1.call-start = ((), (), s32[]{:S(2)}) async-start(), calls=%async_computation.3 | async-start | bytes 1585152 | tf_op jit(solution)/shard_map/all_gather | solution.py:80
  7.9 287.9 %all-gather.4.cloned.1.call-start = ((), (), s32[]{:S(2)}) async-start(), calls=%async_computation.2 | async-start | bytes 2641920 | tf_op jit(solution)/shard_map/all_gather | solution.py:85
  8.7 59.3 %all-to-all-start = ((bf16[128,4,640]{2,1,0:T(4,128)(2,1)}), bf16[128,4,640]{2,1,0:T(4,128)(2,1)S(1)}, u32[]{:S(2)}, u32[]{:S(2)}) async-start(bf16[128,4,640]{2,1,0:T(4,128)(2,1)} %param.23), calls=%async_computation | async-start | bytes 1310720 | tf_op jit(solution)/shard_map/all_to_all | solution.py:103
  28.2 407.4 %all-gather.8.cloned.1.call-start = ((), (), s32[]{:S(2)}) async-start(), calls=%async_computation.4 | async-start | bytes 1585152 | tf_op jit(solution)/shard_map/all_gather | solution.py:131
  28.9 436.2 %reduce-scatter.2.cloned.1.call-start = ((), (), s32[]{:S(2)}) async-start(), calls=%async_computation.5 | async-start | bytes 655360 | tf_op jit(solution)/shard_map/reduce_scatter | solution.py:135
  301.8 136.7 %copy-start.1 = (bf16[2048]{0:T(1024)(128)(2,1)S(1)}, bf16[2048]{0:T(1024)(128)(2,1)}, u32[]{:S(2)}) copy-start(bf16[2048]{0:T(1024)(128)(2,1)} %param.19) | copy-start | bytes 12292
  301.8 136.7 %copy-start.3 = (s32[128]{0:T(128)S(1)}, s32[128]{0:T(128)}, u32[]{:S(2)}) copy-start(s32[128]{0:T(128)} %param.25) | copy-start | bytes 1540
  301.8 137.3 %copy-start.2 = (bf16[64]{0:T(256)(128)(2,1)S(1)}, bf16[64]{0:T(256)(128)(2,1)}, u32[]{:S(2)}) copy-start(bf16[64]{0:T(256)(128)(2,1)} %param.18) | copy-start | bytes 388
Sparse Core Ops, SparseCore 0:
  11.0 144.3 all-gather.5
  158.5 137.2 all-gather.3
  298.8 136.6 all-gather.7
  438.6 26.5 reduce-scatter.1
where the time goes:
time: 475 us; the launch traced here: 474 us
  waiting for transfers between devices  417 us (88%)
  starting transfers between devices  19.7 us (4%)
  between operations  14.1 us (3%)
  other arithmetic  8.47 us (2%)
  local copies, waits for them, and re-layouts  8.03 us (2%)
  matrix products  7.37 us (2%)
    all_gather x1, waiting for transfers between devices, shards(): lax.all_gather(w_keyval, 'seq', axis=0, tiled=True)  136 us
    all_gather x1, waiting for transfers between devices, shards(): lax.all_gather(w_out, 'seq', axis=1, tiled=True)  134 us
    all_gather x1, waiting for transfers between devices, shards(): lax.all_gather(w_query, 'seq', axis=0, tiled=True)  87.2 us
    all_to_all x1, waiting for transfers between devices, shards(): lax.all_to_all(prior_cache, 'seq', split_axis=0, concat_axis=1, tiled=True)  33.9 us
    reduce_scatter x1, waiting for transfers between devices, shards(): lax.psum_scatter(terms.reshape(local_requests, length, width).astype(jnp....  23.6 us
    all_to_all x1, starting transfers between devices, shards(): lax.all_to_all(prior_cache, 'seq', split_axis=0, concat_axis=1, tiled=True)  19.5 us
  transfers between devices with their start and end apart: 5, of which 5 were waited for; matrix products, arithmetic and copies ran while one was open for 4% of the time, Pallas kernels for 0%

commit v1 on v0

--- a/solution.py
+++ b/solution.py
@@ -8,6 +8,18 @@
 QH = 20
 KVH = 5
 epsilon = 1e-06
+
+
+def lift_keys_by_axis(here_x, axis_tag):
+    return jnp.concatenate(
+        lax.all_to_all(
+            jnp.stack(tuple((here_x for _ in range(lax.psum(1, axis_tag)))), 0),
+            axis_name=axis_tag,
+            split_axis=0,
+            concat_axis=0,
+        ),
+        axis=1,
+    )
 
 
 def rms_norm(values, gain):
@@ -126,11 +138,7 @@
         score_scale,
     )
     results = mixed.astype(jnp.bfloat16).reshape(length, local_heads * HD)
-    terms = jnp.dot(
-        results,
-        lax.all_gather(w_out, "seq", axis=1, tiled=True),
-        preferred_element_type=jnp.float32,
-    )
+    terms = jnp.dot(results, lift_keys_by_axis(w_out, "seq"), preferred_element_type=jnp.float32)
     share_rows = length // head_count
     summed = lax.psum_scatter(
         terms.reshape(local_requests, length, width).astype(jnp.bfloat16),

time: 475 us -> 350 us (0.74)
  waiting for transfers between devices: 417 us -> 275 us
  starting transfers between devices: 19.7 us -> 26.6 us
  local copies, waits for them, and re-layouts: 8.03 us -> 13.5 us
    all_gather x1 -> x0, waiting for transfers between devices: 134 us -> none  [shards(): lax.all_gather(w_out, 'seq', axis=1, tiled=True)]
    all_to_all x0 -> x1, starting transfers between devices: none -> 6.95 us  [lift_keys_by_axis(): lax.all_to_all(jnp.stack(tuple((here_x for _ in range(lax.psum(1, axis_ta...]
    all_gather x1, waiting for transfers between devices: 136 us -> 131 us  [shards(): lax.all_gather(w_keyval, 'seq', axis=0, tiled=True)]
  transfers between devices with their start and end apart: 5 -> 5, of which waited for: 5 -> 4; matrix products, arithmetic and copies ran while one was open for 4% -> 8% of each run, Pallas kernels for 0% -> 0%
where the time goes in v1:
time: 350 us; the launch traced here: 349 us
  waiting for transfers between devices  275 us (79%)
  starting transfers between devices  26.6 us (8%)
  between operations  14.2 us (4%)
  local copies, waits for them, and re-layouts  13.5 us (4%)
  other arithmetic  11.2 us (3%)
  matrix products  8.7 us (2%)
    all_gather x1, waiting for transfers between devices, shards(): lax.all_gather(w_keyval, 'seq', axis=0, tiled=True)  131 us
    all_gather x1, waiting for transfers between devices, shards(): lax.all_gather(w_query, 'seq', axis=0, tiled=True)  82.6 us
    all_to_all x1, waiting for transfers between devices, shards(): lax.all_to_all(prior_cache, 'seq', split_axis=0, concat_axis=1, tiled=True)  37.7 us
    reduce_scatter x1, waiting for transfers between devices, shards(): lax.psum_scatter(terms.reshape(local_requests, length, width).astype(jnp....  22.9 us
    all_to_all x1, starting transfers between devices, shards(): lax.all_to_all(prior_cache, 'seq', split_axis=0, concat_axis=1, tiled=True)  19.5 us
  transfers between devices with their start and end apart: 5, of which 4 were waited for; matrix products, arithmetic and copies ran while one was open for 8% of the time, Pallas kernels for 0%

profile of v1, /device:TPU:2, one launch (start us, length us, event | category | flops | bytes accessed | tf_op | source)
XLA Modules:
  0.0 349.4 jit_solution(8276663672337080145)
XLA Ops:
  7.9 19.5 %all-to-all-start = ((bf16[128,4,640]{2,1,0:T(4,128)(2,1)}), bf16[128,4,640]{2,1,0:T(4,128)(2,1)S(1)}, u32[]{:S(2)}, u32[]{:S(2)}) async-start(bf16[128,4,640]{2,1,0:T(4,128)(2,1)} %param.23), calls=%async_computation | async-start | bytes 1310720 | tf_op jit(solution)/shard_map/all_to_all | solution.py:115
  27.5 0.7 all-gather.3.cloned.1.call-update
  28.2 1.2 dynamic_slice.17
  29.5 37.7 %all-to-all-done = bf16[128,4,640]{2,1,0:T(4,128)(2,1)S(1)} async-done(((bf16[128,4,640]{2,1,0:T(4,128)(2,1)}), bf16[128,4,640]{2,1,0:T(4,128)(2,1)S(1)}, u32[]{:S(2)}, u32[]{:S(2)}) %all-to-all-start) | async-done | bytes 655392 | tf_op jit(solution)/shard_map/all_to_all | solution.py:115
  67.2 2.0 stack.2
  69.2 7.0 %all-to-all-start.1 = ((bf16[128,320,16]{1,2,0:T(8,128)(2,1)}), bf16[128,320,16]{1,2,0:T(8,128)(2,1)S(1)}, u32[]{:S(2)}, u32[]{:S(2)}) async-start(bf16[128,320,16]{1,2,0:T(8,128)(2,1)} %stack.2), calls=%async_computation.1 | async-start | bytes 3145728 | tf_op jit(solution)/shard_map/all_to_all | solution.py:15
  78.7 82.6 %all-gather.5.cloned.1.call-done = bf16[2048,320]{1,0:T(8,128)(2,1)} async-done(((bf16[16,320]{1,0:T(8,128)(2,1)}), bf16[2048,320]{1,0:T(8,128)(2,1)}) %all-gather.5.cloned.1.call-update) | async-done | bytes 1310736 | tf_op jit(solution)/shard_map/all_gather | solution.py:92
  161.3 2.6 copy.42
  164.0 0.9 fusion.48
  165.1 1.1 copy.43
  167.5 2.1 multiply_reduce_fusion.2
  171.0 1.0 fusion.30
  172.0 130.7 %all-gather.3.cloned.1.call-done = bf16[2048,640]{1,0:T(8,128)(2,1)} async-done(((bf16[16,640]{1,0:T(8,128)(2,1)}), bf16[2048,640]{1,0:T(8,128)(2,1)}) %all-gather.3.cloned.1.call-update) | async-done | bytes 2621456 | tf_op jit(solution)/shard_map/all_gather | solution.py:97
  302.7 2.9 fusion.17
  306.4 0.7 slice_negate_fusion
  308.5 0.7 fusion.41
  309.2 1.7 fusion.49
  312.0 1.5 fusion
  314.9 0.7 constant_dynamic-slice_fusion
  315.6 0.8 fusion.36
  316.5 0.7 copy.45
  317.2 22.9 %reduce-scatter.2.cloned.1.call-done = bf16[1,32,2048]{2,1,0:T(8,128)(2,1)} async-done(((bf16[1,128,2048]{2,1,0:T(8,128)(2,1)}), bf16[1,32,2048]{2,1,0:T(8,128)(2,1)}) %reduce-scatter.2.cloned.1.call-update) | async-done | bytes 131088 | tf_op jit(solution)/shard_map/reduce_scatter | solution.py:143
  340.1 1.1 multiply_reduce_fusion
  341.2 1.7 select_convert_fusion
  (80 shorter events, 10.7 us)
Async XLA Ops:
  7.2 154.2 %all-gather.5.cloned.1.call-start = ((), (), s32[]{:S(2)}) async-start(), calls=%async_computation.4 | async-start | bytes 1585152 | tf_op jit(solution)/shard_map/all_gather | solution.py:92
  7.9 59.3 %all-to-all-start = ((bf16[128,4,640]{2,1,0:T(4,128)(2,1)}), bf16[128,4,640]{2,1,0:T(4,128)(2,1)S(1)}, u32[]{:S(2)}, u32[]{:S(2)}) async-start(bf16[128,4,640]{2,1,0:T(4,128)(2,1)} %param.23), calls=%async_computation | async-start | bytes 1310720 | tf_op jit(solution)/shard_map/all_to_all | solution.py:115
  27.4 275.3 %all-gather.3.cloned.1.call-start = ((), (), s32[]{:S(2)}) async-start(), calls=%async_computation.3 | async-start | bytes 2641920 | tf_op jit(solution)/shard_map/all_gather | solution.py:97
  29.5 141.6 %copy-start.10 = (pred[5]{0:T(512)(128)(4,1)}, pred[5]{0:T(512)(128)(4,1)S(1)}, u32[]{:S(2)}) copy-start(pred[5]{0:T(512)(128)(4,1)S(1)} %compare_and_fusion) | copy-start | bytes 19
  69.2 7.7 %copy-start.12 = (bf16[64]{0:T(256)(128)(2,1)S(1)}, bf16[64]{0:T(256)(128)(2,1)}, u32[]{:S(2)}) copy-start(bf16[64]{0:T(256)(128)(2,1)} %param.18) | copy-start | bytes 388
  69.2 7.7 %copy-start.14 = (bf16[64]{0:T(256)(128)(2,1)S(1)}, bf16[64]{0:T(256)(128)(2,1)}, u32[]{:S(2)}) copy-start(bf16[64]{0:T(256)(128)(2,1)} %param.17) | copy-start | bytes 388
  69.2 7.7 %copy-start.8 = (bf16[2048]{0:T(1024)(128)(2,1)S(1)}, bf16[2048]{0:T(1024)(128)(2,1)}, u32[]{:S(2)}) copy-start(bf16[2048]{0:T(1024)(128)(2,1)} %param.16) | copy-start | bytes 12292
  69.2 8.6 %copy-start = (bf16[1,128,2048]{2,1,0:T(8,128)(2,1)S(1)}, bf16[1,128,2048]{2,1,0:T(8,128)(2,1)}, u32[]{:S(2)}) copy-start(bf16[1,128,2048]{2,1,0:T(8,128)(2,1)} %param.15) | copy-start | bytes 1572868
  69.2 242.8 %all-to-all-start.1 = ((bf16[128,320,16]{1,2,0:T(8,128)(2,1)}), bf16[128,320,16]{1,2,0:T(8,128)(2,1)S(1)}, u32[]{:S(2)}, u32[]{:S(2)}) async-start(bf16[128,320,16]{1,2,0:T(8,128)(2,1)} %stack.2), calls=%async_computation.1 | async-start | bytes 3145728 | tf_op jit(solution)/shard_map/all_to_all | solution.py:15
  76.1 264.0 %reduce-scatter.2.cloned.1.call-start = ((), (), s32[]{:S(2)}) async-start(), calls=%async_computation.5 | async-start | bytes 655360 | tf_op jit(solution)/shard_map/reduce_scatter | solution.py:143
  76.9 229.4 %copy-start.11 = (f32[64]{0:T(128)}, f32[64]{0:T(128)S(1)}, u32[]{:S(2)}) copy-start(f32[64]{0:T(128)S(1)} %convert_element_type.110) | copy-start | bytes 772
  77.6 228.0 %copy-start.7 = (s32[1024]{0:T(1024)}, s32[1024]{0:T(1024)S(1)}, u32[]{:S(2)}) copy-start(s32[1024]{0:T(1024)S(1)} %pad_clamp_fusion) | copy-start | bytes 12292
  167.4 135.3 %copy-start.1 = (bf16[1,128,2048]{2,1,0:T(8,128)(2,1)S(1)}, bf16[1,128,2048]{2,1,0:T(8,128)(2,1)}, u32[]{:S(2)}) copy-start(bf16[1,128,2048]{2,1,0:T(8,128)(2,1)} %param.15) | copy-start | bytes 1572868
  169.7 0.7 copy-start.2
  306.3 0.8 copy-start.6
  309.2 2.2 copy-start.3
  312.0 1.6 copy-start.15
  312.0 2.1 copy-start.13
  312.0 2.2 copy-start.9
  312.0 3.6 %copy-start.4 = (f32[128,5,32]{0,2,1:T(8,128)S(1)}, f32[128,5,32]{0,2,1:T(8,128)}, u32[]{:S(2)}) copy-start(f32[128,5,32]{0,2,1:T(8,128)} %get-tuple-element.18) | copy-start | bytes 245764
  312.0 3.6 %copy-start.5 = (f32[128,5,32]{0,2,1:T(8,128)S(1)}, f32[128,5,32]{0,2,1:T(8,128)}, u32[]{:S(2)}) copy-start(f32[128,5,32]{0,2,1:T(8,128)} %get-tuple-element.21) | copy-start | bytes 245764
Sparse Core Ops, SparseCore 0:
  11.0 150.2 all-gather.4
  164.4 138.2 all-gather.2
  313.6 26.4 reduce-scatter.1
